TPU v7x, 128 devices: a whole 4x4x4 slice. The times are simulated.
128 devices in a mesh: cd: 8 (over x_hi, y), ab: 16 (over z, x_lo, core).
Axes of the slice: x: 4 (x_hi: 2, x_lo: 2; x = x_hi * 2 + x_lo), y: 4, z: 4, core: 2. Of those that a mesh axis runs over, the one named last changes fastest.
Arguments:
- amplitudes: float32 [1024, 16384], P('ab', 'cd'), may hold values from -6 to 6
- singles: float32 [256, 1024], replicated, may hold values from -3 to 3
- pair_list: int32 [1024, 2], P('ab'), may hold values from 0 to 255
- irrep: int32 [1024], replicated, may hold values from 0 to 7
- block_sizes: int32 [16], replicated, may hold values from 1 to 2, 24 in all
- tile_of_slot: int32 [32], replicated, may hold values from 0 to 511
- integrals: bfloat16 [65536, 16384], P('ab', 'cd'), may hold values from -0.125 to 0.125
Outputs:
- residual: float32 [1024, 65536], P('cd', 'ab')
Inputs may be any that keep to these rules, and one draw needn't show every extreme that they name: `block_sizes`: the live slots of an index of ab are its leading ones; the entries sum to 24. `tile_of_slot`: tile t holds the ab pairs whose first orbital is 2 t or 2 t + 1.
All inputs are finite; a program needn't handle non-finite values.
Results may differ from a plain program's by a relative error of at most 0.0029.
Values may be sent and summed in bfloat16 or wider, within the bound.
A program may use at most 128 MiB of HBM per device.

v0:
```python
import jax
import jax.numpy as jnp
from jax import lax
from jax.sharding import PartitionSpec as P


def tile_symmetry(tiles, rows, irrep):
    orbitals = irrep.shape[0]
    table = jnp.arange(orbitals, dtype=jnp.int32)
    first = jnp.sum(jnp.where(table[None, :] == 2 * tiles[:, None], irrep[None, :], 0), axis=1)
    second = jnp.sum(jnp.where(table[None, :] == 2 * tiles[:, None] + 1, irrep[None, :], 0), axis=1)
    upper = (rows // orbitals)[None, :]
    leading = jnp.where(upper == 0, first[:, None], second[:, None])
    trailing = jnp.take(irrep, rows % orbitals)
    return jnp.bitwise_xor(leading, trailing[None, :])


def on_device(amplitudes, singles, pair_list, irrep, block_sizes, tile_of_slot, integrals):
    groups = lax.axis_size("ab")
    owner_index = lax.axis_index("ab")
    slab_index = lax.axis_index("cd")
    orbitals = irrep.shape[0]
    columns = amplitudes.shape[1]
    slab = columns // orbitals
    local_pairs = amplitudes.shape[0]
    left = jnp.take(singles, pair_list[:, 0], axis=0)
    left = lax.dynamic_slice_in_dim(left, slab_index * slab, slab, 1)
    right = jnp.take(singles, pair_list[:, 1], axis=0)
    combined = amplitudes + (left[:, :, None] * right[:, None, :]).reshape(local_pairs, columns)
    combined_low = combined.astype(jnp.bfloat16)
    slab_irrep = lax.dynamic_slice_in_dim(irrep, slab_index * slab, slab, 0)
    column_irrep = jnp.bitwise_xor(slab_irrep[:, None], irrep[None, :]).reshape(columns)
    capacity = tile_of_slot.shape[0] // groups
    tile_rows = integrals.shape[0] // capacity
    zero_low = jnp.zeros((), jnp.bfloat16)
    count = jnp.take(block_sizes, owner_index)
    tiles = lax.dynamic_slice_in_dim(tile_of_slot, owner_index * capacity, capacity, 0)
    symmetry = tile_symmetry(tiles, jnp.arange(tile_rows, dtype=jnp.int32), irrep)
    masked = jnp.where(
        symmetry[:, :, None] == column_irrep[None, None, :],
        integrals.reshape(capacity, tile_rows, columns),
        zero_low,
    )
    piece = lax.all_gather(combined_low, "ab", axis=0, tiled=True)

    def add_slot(index, result):
        weights = lax.dynamic_index_in_dim(masked, index, 0, keepdims=False)
        product = lax.dot_general(
            piece, weights, (((1,), (1,)), ((), ())), preferred_element_type=jnp.float32
        )
        return lax.dynamic_update_slice_in_dim(result, product[:, None, :], index, 1)

    result = jnp.zeros((piece.shape[0], capacity, tile_rows), jnp.float32)
    result = lax.fori_loop(0, count, add_slot, result)
    partial_value = result.reshape(piece.shape[0], capacity * tile_rows)
    summed = lax.psum_scatter(partial_value, "cd", scatter_dimension=0, tiled=True)
    return summed


def solution(mesh):
    placed = (P("ab", "cd"), P(), P("ab", None), P(), P(), P(), P("ab", "cd"))
    return jax.shard_map(
        on_device, mesh=mesh, in_specs=placed, out_specs=P("cd", "ab"), check_vma=False
    )
```

profile of v0, /device:TPU:0, one launch (start us, length us, event | category | flops | bytes accessed | tf_op | source)
XLA Modules:
  0.0 305.4 jit_solution(1114060148061859263)
XLA Ops:
  6.5 0.0 copy-start
  6.5 0.0 all-gather.2.cloned.1.call-start
  6.5 0.8 compare_and_fusion.1
  7.3 0.5 copy-done
  7.8 0.7 gather_fusion.2
  8.5 0.7 gather_fusion.1
  9.2 0.1 broadcast_select_fusion
  9.2 0.1 dynamic-slice_select_fusion
  9.3 0.2 broadcast_multiply_fusion
  9.6 0.2 copy.13
  9.8 1.8 add_convert_fusion
  11.6 0.0 all-gather.2.cloned.1.call-update
  11.6 0.0 reduce-scatter.2.cloned.1.call-start
  11.7 1.3 dynamic-slice.2
  13.0 0.8 dynamic_slice.14
  13.7 0.7 broadcast_add_fusion
  14.4 0.9 fusion.13
  15.4 10.2 %gather_fusion = s32[2048]{0:T(1024)S(1)} fusion(s32[1024]{0:T(1024)} %param.14, s32[2048]{0:T(1024)S(1)} %broadcast_clamp_fusion), kind=kCustom, calls=%fused_computation.2 | custom fusion | bytes 24576 | tf_op jit(solution)/shard_map/jit(_take)/gather | solution.py:14
  26.3 0.1 select_xor_fusion
  26.4 15.3 %compare_select_fusion = bf16[2,2048,2048]{2,1,0:T(8,128)(2,1)} fusion(bf16[2,2048,2048]{2,1,0:T(8,128)(2,1)} %bitcast.35, s32[2048]{0:T(1024)S(1)} %bitcast.38, s32[2,2048]{1,0:T(2,128)S(1)} %select_xor_fusion), kind=kLoop, calls=%fused_computation.8 | loop fusion | flops 16777216 | bytes 33579008 | tf_op jit(solution)/shard_map/jit(_where)/select_n | solution.py:39
  41.6 10.0 %all-gather.2.cloned.1.call-done = bf16[1024,2048]{1,0:T(8,128)(2,1)} async-done(((bf16[64,2048]{1,0:T(8,128)(2,1)}), bf16[1024,2048]{1,0:T(8,128)(2,1)}) %all-gather.2.cloned.1.call-update) | async-done | bytes 4194320 | tf_op jit(solution)/shard_map/all_gather | solution.py:44
  51.7 7.9 %broadcast_in_dim.84 = f32[1024,2,2048]{0,2,1:T(8,128)} broadcast(f32[]{:T(128)} %constant.87.clone.1), dimensions={} | broadcast | bytes 16777220 | tf_op jit(solution)/shard_map/broadcast_in_dim | solution.py:53
  59.5 29.0 %while.11 = (s32[]{:T(128)}, f32[1024,2,2048]{0,2,1:T(8,128)}, s32[]{:T(128)}, bf16[2,2048,2048]{2,1,0:T(8,128)(2,1)}, bf16[1024,2048]{1,0:T(8,128)(2,1)}, /*index=5*/s32[]{:T(128)}, s32[]{:T(128)}, s32[]{:T(128)}) while((s32[]{:T(128)}, f32[1024,2,2048]{0,2,1:T(8,128)}, s32[]{:T(128)}, bf16[2,2048,2048]{2,1,0:T(8,128)(2,1)}, ...), condition=%wide.region_3.5_spmd, body=%wide.region_2.4_spmd.sunk | while | flops 8589934592 | bytes 20972672 | solution.py:54
  59.5 14.5 %bitcast_dynamic-update-slice_fusion.2 = f32[1024,2,2048]{0,2,1:T(8,128)} fusion(f32[1024,2,2048]{0,2,1:T(8,128)} %get-tuple-element.110, s32[]{:T(128)S(6)} %select_n.156, bf16[1024,2048]{1,0:T(8,128)(2,1)} %get-tuple-element.121, bf16[2,2048,2048]{2,1,0:T(8,128)(2,1)} %get-tuple-element.120), kind=kOutput, calls=%fused_computation.3.clone.1 | convolution fusion | flops 8589934592 | bytes 20972544 | tf_op jit(solution)/shard_map/while/body/dot_general | solution.py:48
  74.0 14.5 %bitcast_dynamic-update-slice_fusion.2 = f32[1024,2,2048]{0,2,1:T(8,128)} fusion(f32[1024,2,2048]{0,2,1:T(8,128)} %get-tuple-element.110, s32[]{:T(128)S(6)} %select_n.156, bf16[1024,2048]{1,0:T(8,128)(2,1)} %get-tuple-element.121, bf16[2,2048,2048]{2,1,0:T(8,128)(2,1)} %get-tuple-element.120), kind=kOutput, calls=%fused_computation.3.clone.1 | convolution fusion | flops 8589934592 | bytes 20972544 | tf_op jit(solution)/shard_map/while/body/dot_general | solution.py:48
  88.5 0.0 copy-start.1
  88.5 17.6 %copy.11 = f32[1024,4096]{1,0:T(8,128)} copy(f32[1024,4096]{0,1:T(8,128)} %bitcast.34) | data formatting | bytes 33554432 | tf_op jit(solution)/shard_map/reshape | solution.py:55
  106.0 0.0 reduce-scatter.2.cloned.1.call-update
  106.1 192.4 %reduce-scatter.2.cloned.1.call-done = f32[128,4096]{1,0:T(8,128)} async-done(((f32[1024,4096]{1,0:T(8,128)}), f32[128,4096]{1,0:T(8,128)}) %reduce-scatter.2.cloned.1.call-update) | async-done | bytes 2097168 | tf_op jit(solution)/shard_map/reduce_scatter | solution.py:56
  298.5 0.0 copy-done.1
  (6 shorter events, 0.0 us)
Async XLA Ops:
  6.5 1.3 copy-start
  6.5 45.1 %all-gather.2.cloned.1.call-start = ((), (), s32[]{:S(2)}) async-start(), calls=%async_computation.1 | async-start | bytes 4456448 | tf_op jit(solution)/shard_map/all_gather | solution.py:44
  11.6 286.9 %reduce-scatter.2.cloned.1.call-start = ((), (), s32[]{:S(2)}) async-start(), calls=%async_computation.2 | async-start | bytes 18874368 | tf_op jit(solution)/shard_map/reduce_scatter | solution.py:56
  88.5 210.0 %copy-start.1 = (f32[256,1024]{1,0:T(8,128)S(1)}, f32[256,1024]{1,0:T(8,128)}, u32[]{:S(2)}) copy-start(f32[256,1024]{1,0:T(8,128)} %param.12) | copy-start | bytes 3145732
Sparse Core Ops, SparseCore 0:
  11.7 39.8 all-gather.1
  106.2 192.2 reduce-scatter.1
where the time goes:
time: 306 us; the launch traced here: 305 us
  waiting for transfers between devices  203 us (66%)
  local copies, waits for them, and re-layouts  39.7 us (13%)
  matrix products  29 us (9%)
  other arithmetic  20.1 us (7%)
  between operations  14.1 us (5%)
    reduce_scatter x1, waiting for transfers between devices, on_device(): lax.psum_scatter(partial_value, 'cd', scatter_dimension=0, tiled=True)  192 us
    dot_general x2, matrix products, add_slot(): lax.dot_general(piece, weights, (((1,), (1,)), ((), ())), preferred_eleme...  29 us
    reshape x1, local copies, waits for them, and re-layouts, on_device(): partial_value = result.reshape(piece.shape[0], capacity * tile_rows)  17.6 us
    select_n x1, other arithmetic, on_device(): jnp.where(symmetry[:, :, None] == column_irrep[None, None, :], integrals....  15.3 us
    gather x1, local copies, waits for them, and re-layouts, tile_symmetry(): trailing = jnp.take(irrep, rows % orbitals)  10.2 us
    all_gather x1, waiting for transfers between devices, on_device(): piece = lax.all_gather(combined_low, 'ab', axis=0, tiled=True)  10 us
    broadcast_in_dim x1, local copies, waits for them, and re-layouts, on_device(): result = jnp.zeros((piece.shape[0], capacity, tile_rows), jnp.float32)  7.86 us
  transfers between devices with their start and end apart: 2, of which 2 were waited for; matrix products, arithmetic and copies ran while one was open for 10% of the time, Pallas kernels for 0%

commit v1 on v0

v1 whole, which is shorter than its diff:
```python
import functools

import jax
import jax.numpy as jnp
from jax import lax
from jax.experimental import pallas as pl
from jax.experimental.pallas import tpu as pltpu
from jax.sharding import PartitionSpec as P

MESH = pl.DeviceIdType.MESH
KINDS = 7


def tile_symmetry(tiles, rows, irrep):
    orbitals = irrep.shape[0]
    table = jnp.arange(orbitals, dtype=jnp.int32)
    first = jnp.sum(jnp.where(table[None, :] == 2 * tiles[:, None], irrep[None, :], 0), axis=1)
    second = jnp.sum(jnp.where(table[None, :] == 2 * tiles[:, None] + 1, irrep[None, :], 0), axis=1)
    upper = (rows // orbitals)[None, :]
    leading = jnp.where(upper == 0, first[:, None], second[:, None])
    trailing = jnp.take(irrep, rows % orbitals)
    return jnp.bitwise_xor(leading, trailing[None, :])


def ladder_kernel(
    ring, width, inner,
    tau_any, tiles_any, row_ref, column_ref, out_ref,
    tau, tiles, acc, keep, sent, held,
    tau_sem, tile_sem, send_sem, recv_sem,
):
    chunks = tiles.shape[0]
    rows = out_ref.shape[0]
    me = lax.axis_index("cd")
    y, x = lax.rem(me, ring), lax.div(me, ring)
    up_y, down_y, far_y = lax.rem(y + 1, ring), lax.rem(y + ring - 1, ring), lax.rem(y + 2, ring)
    up, down, across = x * ring + up_y, x * ring + down_y, (1 - x) * ring + y
    targets = (up, down, up, down, up, down, across)

    tau_copy = pltpu.make_async_copy(tau_any, tau, tau_sem)
    tau_copy.start()

    def tile_copy(c):
        return pltpu.make_async_copy(
            tiles_any.at[pl.ds(pl.multiple_of(c * width, width), width), :], tiles.at[c], tile_sem.at[c]
        )

    def remote(kind, c):
        return pltpu.make_async_remote_copy(
            src_ref=sent.at[kind, c],
            dst_ref=held.at[kind, c],
            send_sem=send_sem.at[kind, c],
            recv_sem=recv_sem.at[kind, c],
            device_id={"cd": targets[kind]},
            device_id_type=MESH,
        )

    @pl.loop(0, chunks)
    def _(c):
        tile_copy(c).start()

    barrier = pltpu.get_barrier_semaphore()
    for other in (up, down, across):
        pl.semaphore_signal(barrier, inc=1, device_id={"cd": other}, device_id_type=MESH)
    pl.semaphore_wait(barrier, 3)
    tau_copy.wait()

    def piece(part, block):
        return acc[pl.ds(pl.multiple_of((part * ring + block) * rows, rows), rows), :]

    def multiply(c):
        tile_copy(c).wait()

        @pl.loop(0, width // inner)
        def _(t):
            at = pl.multiple_of(t * inner, inner)
            row = row_ref[pl.ds(pl.multiple_of(c * width + t * inner, inner), inner), :]
            tile = tiles[c, pl.ds(at, inner), :]
            masked = jnp.where(row == column_ref[...], tile, jnp.zeros_like(tile))
            acc[:, pl.ds(at, inner)] = lax.dot_general(
                tau[...], masked, (((1,), (1,)), ((), ())), preferred_element_type=jnp.float32
            )

        for kind, part, block in ((0, 0, far_y), (1, 1, far_y), (2, 1, up_y), (3, 0, down_y)):
            sent[kind, c] = piece(part, block).astype(jnp.bfloat16)
            remote(kind, c).start()
        for slot, part, block in ((0, 0, up_y), (1, 1, down_y), (2, 0, y), (3, 1, y)):
            keep[slot, c] = piece(part, block)

    def relay(c):
        for kind in (0, 1):
            remote(kind, c).wait_recv()
            total = keep[kind, c] + held[kind, c].astype(jnp.float32)
            sent[4 + kind, c] = total.astype(jnp.bfloat16)
            remote(4 + kind, c).start()

    def cross(c):
        for kind in (2, 3, 4, 5):
            remote(kind, c).wait_recv()
        first = keep[2, c] + held[3, c].astype(jnp.float32) + held[4, c].astype(jnp.float32)
        second = keep[3, c] + held[2, c].astype(jnp.float32) + held[5, c].astype(jnp.float32)
        sent[6, c] = jnp.where(x == 0, second, first).astype(jnp.bfloat16)
        remote(6, c).start()
        keep[2, c] = jnp.where(x == 0, first, second)

    def finish(c):
        remote(6, c).wait_recv()
        at = pl.multiple_of(c * width, width)
        out_ref[:, pl.ds(at, width)] = keep[2, c] + held[6, c].astype(jnp.float32)

    @pl.loop(0, chunks + 3)
    def _(i):
        for lag, stage in enumerate((multiply, relay, cross, finish)):
            @pl.when((i >= lag) & (i < chunks + lag))
            def _():
                stage(i - lag)

    @pl.loop(0, chunks)
    def _(c):
        for kind in range(KINDS):
            remote(kind, c).wait_send()


def ladder(ring, tau, integrals, row_symmetry, column_symmetry, width, inner):
    pairs, columns = tau.shape
    rows = pairs // (2 * ring)
    total = integrals.shape[0]
    chunks = total // width
    anywhere = pl.BlockSpec(memory_space=pl.ANY)
    local = pl.BlockSpec(memory_space=pltpu.VMEM)
    return pl.pallas_call(
        functools.partial(ladder_kernel, ring, width, inner),
        out_shape=jax.ShapeDtypeStruct((rows, total), jnp.float32),
        in_specs=[anywhere, anywhere, local, local],
        out_specs=local,
        scratch_shapes=[
            pltpu.VMEM((pairs, columns), jnp.bfloat16),
            pltpu.VMEM((chunks, width, columns), jnp.bfloat16),
            pltpu.VMEM((pairs, width), jnp.float32),
            pltpu.VMEM((4, chunks, rows, width), jnp.float32),
            pltpu.VMEM((KINDS, chunks, rows, width), jnp.bfloat16),
            pltpu.VMEM((KINDS, chunks, rows, width), jnp.bfloat16),
            pltpu.SemaphoreType.DMA,
            pltpu.SemaphoreType.DMA((chunks,)),
            pltpu.SemaphoreType.DMA((KINDS, chunks)),
            pltpu.SemaphoreType.DMA((KINDS, chunks)),
        ],
        compiler_params=pltpu.CompilerParams(
            collective_id=0, has_side_effects=True, vmem_limit_bytes=60 * 1024 * 1024
        ),
    )(tau, integrals, row_symmetry, column_symmetry)


def on_device(amplitudes, singles, pair_list, irrep, block_sizes, tile_of_slot, integrals):
    groups = lax.axis_size("ab")
    ring = lax.axis_size("cd") // 2
    owner_index = lax.axis_index("ab")
    slab_index = lax.axis_index("cd")
    orbitals = irrep.shape[0]
    columns = amplitudes.shape[1]
    slab = columns // orbitals
    local_pairs = amplitudes.shape[0]
    left = jnp.take(singles, pair_list[:, 0], axis=0)
    left = lax.dynamic_slice_in_dim(left, slab_index * slab, slab, 1)
    right = jnp.take(singles, pair_list[:, 1], axis=0)
    combined = amplitudes + (left[:, :, None] * right[:, None, :]).reshape(local_pairs, columns)
    combined_low = combined.astype(jnp.bfloat16)
    piece = lax.all_gather(combined_low, "ab", axis=0, tiled=True)
    slab_irrep = lax.dynamic_slice_in_dim(irrep, slab_index * slab, slab, 0)
    column_irrep = jnp.bitwise_xor(slab_irrep[:, None], irrep[None, :]).reshape(1, columns)
    capacity = tile_of_slot.shape[0] // groups
    tile_rows = integrals.shape[0] // capacity
    count = jnp.take(block_sizes, owner_index)
    tiles = lax.dynamic_slice_in_dim(tile_of_slot, owner_index * capacity, capacity, 0)
    symmetry = tile_symmetry(tiles, jnp.arange(tile_rows, dtype=jnp.int32), irrep)
    live = jnp.arange(capacity, dtype=jnp.int32)[:, None] < count
    symmetry = jnp.where(live, symmetry, -1).reshape(capacity * tile_rows, 1)
    width = min(512, tile_rows // 2)
    return ladder(
        ring, piece, integrals,
        symmetry.astype(jnp.bfloat16), column_irrep.astype(jnp.bfloat16),
        width, min(256, width),
    )


def solution(mesh):
    placed = (P("ab", "cd"), P(), P("ab", None), P(), P(), P(), P("ab", "cd"))
    return jax.shard_map(
        on_device, mesh=mesh, in_specs=placed, out_specs=P("cd", "ab"), check_vma=False
    )
```

time: 306 us -> 148 us (0.48)
  waiting for transfers between devices: 203 us -> 27.5 us
  Pallas kernels: 0 us -> 86.9 us
  matrix products: 29 us -> 0 us
  local copies, waits for them, and re-layouts: 39.7 us -> 16.4 us
  other arithmetic: 20.1 us -> 2.41 us
    reduce_scatter x1 -> x0, waiting for transfers between devices: 192 us -> none  [on_device(): lax.psum_scatter(partial_value, 'cd', scatter_dimension=0, tiled=True)]
    pallas_call x0 -> x1, Pallas kernels: none -> 86.9 us  [ladder(): pl.pallas_call(functools.partial(ladder_kernel, ring, width, inner), out_...]
    dot_general x2 -> x0, matrix products: 29 us -> none  [add_slot(): lax.dot_general(piece, weights, (((1,), (1,)), ((), ())), preferred_eleme...]
    reshape x1 -> x0, local copies, waits for them, and re-layouts: 17.6 us -> none  [on_device(): partial_value = result.reshape(piece.shape[0], capacity * tile_rows)]
    all_gather x1, waiting for transfers between devices: 10 us -> 27.5 us  [on_device(): piece = lax.all_gather(combined_low, 'ab', axis=0, tiled=True)]
    select_n x1 -> x0, other arithmetic: 15.3 us -> none  [on_device(): jnp.where(symmetry[:, :, None] == column_irrep[None, None, :], integrals....]
    broadcast_in_dim x1 -> x0, local copies, waits for them, and re-layouts: 7.86 us -> none  [on_device(): result = jnp.zeros((piece.shape[0], capacity, tile_rows), jnp.float32)]
    unnamed x6 -> x15, local copies, waits for them, and re-layouts: 0.62 us -> 5.72 us
  transfers between devices with their start and end apart: 2 -> 1, of which waited for: 2 -> 1; matrix products, arithmetic and copies ran while one was open for 10% -> 8% of each run, Pallas kernels for 0% -> 0%
where the time goes in v1:
time: 148 us; the launch traced here: 147 us
  Pallas kernels  86.9 us (59%)
  waiting for transfers between devices  27.5 us (19%)
  local copies, waits for them, and re-layouts  16.4 us (11%)
  between operations  14.2 us (10%)
  other arithmetic  2.41 us (2%)
    pallas_call x1, Pallas kernels, ladder(): pl.pallas_call(functools.partial(ladder_kernel, ring, width, inner), out_...  86.9 us
    all_gather x1, waiting for transfers between devices, on_device(): piece = lax.all_gather(combined_low, 'ab', axis=0, tiled=True)  27.5 us
    gather x1, local copies, waits for them, and re-layouts, tile_symmetry(): trailing = jnp.take(irrep, rows % orbitals)  8.58 us
    unnamed x15, local copies, waits for them, and re-layouts  5.72 us
  transfers between devices with their start and end apart: 1, of which 1 were waited for; matrix products, arithmetic and copies ran while one was open for 8% of the time, Pallas kernels for 0%

profile of v1, /device:TPU:0, one launch (start us, length us, event | category | flops | bytes accessed | tf_op | source)
XLA Modules:
  0.0 147.4 jit_solution(9233654821872541251)
XLA Ops:
  6.5 0.0 copy-start
  6.5 0.0 copy-start.2
  6.5 0.0 all-gather.2.cloned.1.call-start
  6.5 0.8 compare_and_fusion.1
  7.4 0.4 copy-done
  7.8 0.0 copy-start.4
  7.8 0.0 copy-start.1
  7.8 0.0 copy-start.3
  7.8 0.7 gather_fusion.2
  8.5 0.7 gather_fusion.1
  9.2 0.1 broadcast_select_fusion
  9.3 0.1 dynamic-slice_select_fusion
  9.3 0.2 broadcast_multiply_fusion
  9.6 0.2 copy.9
  9.8 0.0 copy-done.2
  9.8 0.8 add_convert_fusion
  10.5 0.0 all-gather.2.cloned.1.call-update
  10.6 0.0 copy-done.4
  10.6 0.7 dynamic-slice.2
  11.2 0.0 copy-done.1
  11.2 0.1 dynamic_slice.11
  11.3 0.0 copy-done.3
  11.3 0.1 broadcast_add_fusion
  11.4 0.2 fusion.8
  11.6 0.6 copy.12
  12.3 8.6 %gather_fusion = s32[2048]{0:T(1024)S(1)} fusion(s32[1024]{0:T(1024)S(1)} %copy-done.1, s32[2048]{0:T(1024)S(1)} %broadcast_clamp_fusion), kind=kCustom, calls=%fused_computation.2 | custom fusion | bytes 24576 | tf_op jit(solution)/shard_map/jit(_take)/gather | solution.py:21
  21.6 0.1 fusion.6
  21.7 1.4 copy.11
  23.1 27.5 %all-gather.2.cloned.1.call-done.tau_any = bf16[1024,2048]{1,0:T(8,128)(2,1)} async-done(((bf16[64,2048]{1,0:T(8,128)(2,1)}), bf16[1024,2048]{1,0:T(8,128)(2,1)}) %all-gather.2.cloned.1.call-update) | async-done | bytes 4194320 | tf_op jit(solution)/shard_map/all_gather | solution.py:167
  50.6 86.9 %shard_map.73 = f32[128,4096]{1,0:T(8,128)} custom-call(bf16[1024,2048]{1,0:T(8,128)(2,1)} %all-gather.2.cloned.1.call-done.tau_any, bf16[4096,2048]{1,0:T(8,128)(2,1)} %tiles_any.1, bf16[4096,1]{1,0:T(8,128)(2,1)} %bitcast.20, bf16[1,2048]{1,0:T(2,128)(2,1)} %bitcast.24), custom_call_target="tpu_custom_call" | custom-call | tf_op jit(solution)/shard_map/pallas_call | solution.py:130
  137.5 3.1 %copy.14 = f32[128,4096]{1,0:T(8,128)} copy(f32[128,4096]{1,0:T(8,128)} %shard_map.73) | data formatting | bytes 4194304
  (7 shorter events, 0.0 us)
Async XLA Ops:
  6.5 1.3 copy-start
  6.5 3.2 %copy-start.2 = (f32[64,2048]{1,0:T(8,128)S(1)}, f32[64,2048]{1,0:T(8,128)}, u32[]{:S(2)}) copy-start(f32[64,2048]{1,0:T(8,128)} %param.9) | copy-start | bytes 1572868
  6.5 44.1 %all-gather.2.cloned.1.call-start = ((), (), s32[]{:S(2)}) async-start(), calls=%async_computation | async-start | bytes 4456448 | tf_op jit(solution)/shard_map/all_gather | solution.py:167
  7.8 2.8 %copy-start.4 = (s32[16]{0:T(128)S(1)}, s32[16]{0:T(128)}, u32[]{:S(2)}) copy-start(s32[16]{0:T(128)} %param.13) | copy-start | bytes 196
  7.8 3.5 %copy-start.1 = (s32[1024]{0:T(1024)S(1)}, s32[1024]{0:T(1024)}, u32[]{:S(2)}) copy-start(s32[1024]{0:T(1024)} %param.12) | copy-start | bytes 12292
  7.8 3.5 %copy-start.3 = (s32[32]{0:T(128)S(1)}, s32[32]{0:T(128)}, u32[]{:S(2)}) copy-start(s32[32]{0:T(128)} %param.14) | copy-start | bytes 388
Sparse Core Ops, SparseCore 0:
  10.7 39.8 all-gather.1

commit v2 on v1

--- a/solution.py
+++ b/solution.py
@@ -9,6 +9,24 @@
 
 MESH = pl.DeviceIdType.MESH
 KINDS = 7
+HOPS = (
+    ((0, 0, 0), 0, (0, 1, 0)),
+    ((0, 0, 0), 1, (3, 0, 0)),
+    ((0, 0, 0), 2, (1, 0, 0)),
+    ((0, 0, 0), 3, (0, 0, 1)),
+    ((0, 1, 0), 1, (3, 1, 0)),
+    ((0, 1, 0), 2, (1, 1, 0)),
+    ((0, 1, 0), 3, (0, 1, 1)),
+    ((3, 0, 0), 1, (2, 0, 0)),
+    ((3, 0, 0), 3, (3, 0, 1)),
+    ((1, 0, 0), 3, (1, 0, 1)),
+    ((3, 1, 0), 3, (3, 1, 1)),
+    ((1, 1, 0), 2, (2, 1, 0)),
+    ((1, 1, 0), 3, (1, 1, 1)),
+    ((2, 0, 0), 3, (2, 0, 1)),
+    ((2, 1, 0), 3, (2, 1, 1)),
+)
+RELAYS = ((0, (4, 5, 6)), (1, (7, 8)), (2, (9,)), (4, (10,)), (5, (11, 12)), (7, (13,)), (11, (14,)))
 
 
 def tile_symmetry(tiles, rows, irrep):
@@ -18,15 +36,15 @@
     second = jnp.sum(jnp.where(table[None, :] == 2 * tiles[:, None] + 1, irrep[None, :], 0), axis=1)
     upper = (rows // orbitals)[None, :]
     leading = jnp.where(upper == 0, first[:, None], second[:, None])
-    trailing = jnp.take(irrep, rows % orbitals)
+    trailing = jnp.tile(irrep, rows.shape[0] // orbitals)
     return jnp.bitwise_xor(leading, trailing[None, :])
 
 
 def ladder_kernel(
-    ring, width, inner,
-    tau_any, tiles_any, row_ref, column_ref, out_ref,
+    ring, width, inner, parts,
+    own_ref, tiles_any, row_ref, column_ref, out_ref,
     tau, tiles, acc, keep, sent, held,
-    tau_sem, tile_sem, send_sem, recv_sem,
+    tile_sem, send_sem, recv_sem, spread_sem, gather_sem,
 ):
     chunks = tiles.shape[0]
     rows = out_ref.shape[0]
@@ -36,8 +54,41 @@
     up, down, across = x * ring + up_y, x * ring + down_y, (1 - x) * ring + y
     targets = (up, down, up, down, up, down, across)
 
-    tau_copy = pltpu.make_async_copy(tau_any, tau, tau_sem)
-    tau_copy.start()
+    owner = lax.axis_index("ab")
+    z, side, core = lax.div(owner, 4), lax.rem(lax.div(owner, 2), 2), lax.rem(owner, 2)
+    depth = tau.shape[0] // 16 // parts
+
+    def shard(dz, dx, dk):
+        return lax.rem(z + dz, 4) * 4 + lax.rem(side + dx, 2) * 2 + lax.rem(core + dk, 2)
+
+    beside, above, below, twin = shard(0, 1, 0), shard(1, 0, 0), shard(3, 0, 0), shard(0, 0, 1)
+
+    def block(index, part):
+        return pl.ds(pl.multiple_of((index * parts + part) * depth, depth), depth)
+
+    def give(hop, part):
+        offset, other, _ = HOPS[hop]
+        target = (beside, above, below, twin)[other]
+        rows_at = block(shard(*offset), part)
+        source = tau.at[rows_at, :]
+        if offset == (0, 0, 0):
+            source = own_ref.at[pl.ds(part * depth, depth), :]
+        return pltpu.make_async_remote_copy(
+            src_ref=source,
+            dst_ref=tau.at[rows_at, :],
+            send_sem=spread_sem.at[hop, part],
+            recv_sem=gather_sem.at[hop, part],
+            device_id={"ab": target},
+            device_id_type=MESH,
+        )
+
+    def take(hop, part):
+        landed = tau.at[block(shard(*HOPS[hop][2]), part), :]
+        pltpu.make_async_remote_copy(
+            src_ref=landed, dst_ref=landed,
+            send_sem=spread_sem.at[hop, part], recv_sem=gather_sem.at[hop, part],
+            device_id={"ab": beside}, device_id_type=MESH,
+        ).wait_recv()
 
     def tile_copy(c):
         return pltpu.make_async_copy(
@@ -61,8 +112,23 @@
     barrier = pltpu.get_barrier_semaphore()
     for other in (up, down, across):
         pl.semaphore_signal(barrier, inc=1, device_id={"cd": other}, device_id_type=MESH)
-    pl.semaphore_wait(barrier, 3)
-    tau_copy.wait()
+    for other in (beside, above, below, twin):
+        pl.semaphore_signal(barrier, inc=1, device_id={"ab": other}, device_id_type=MESH)
+    pl.semaphore_wait(barrier, 7)
+
+    for hop in (1, 2, 0, 3):
+        for part in range(parts):
+            give(hop, part).start()
+    for part in range(parts):
+        tau[block(owner, part), :] = own_ref[part * depth:(part + 1) * depth, :]
+    for arrived, onward in RELAYS:
+        for part in range(parts):
+            take(arrived, part)
+            for hop in onward:
+                give(hop, part).start()
+    for hop in (3, 6, 8, 9, 10, 12, 13, 14):
+        for part in range(parts):
+            take(hop, part)
 
     def piece(part, block):
         return acc[pl.ds(pl.multiple_of((part * ring + block) * rows, rows), rows), :]
@@ -119,18 +185,22 @@
         for kind in range(KINDS):
             remote(kind, c).wait_send()
 
-
-def ladder(ring, tau, integrals, row_symmetry, column_symmetry, width, inner):
-    pairs, columns = tau.shape
+    for hop in range(len(HOPS)):
+        for part in range(parts):
+            give(hop, part).wait_send()
+
+
+def ladder(ring, own, integrals, row_symmetry, column_symmetry, width, inner, parts):
+    pairs, columns = own.shape[0] * 16, own.shape[1]
     rows = pairs // (2 * ring)
     total = integrals.shape[0]
     chunks = total // width
     anywhere = pl.BlockSpec(memory_space=pl.ANY)
     local = pl.BlockSpec(memory_space=pltpu.VMEM)
     return pl.pallas_call(
-        functools.partial(ladder_kernel, ring, width, inner),
+        functools.partial(ladder_kernel, ring, width, inner, parts),
         out_shape=jax.ShapeDtypeStruct((rows, total), jnp.float32),
-        in_specs=[anywhere, anywhere, local, local],
+        in_specs=[local, anywhere, local, local],
         out_specs=local,
         scratch_shapes=[
             pltpu.VMEM((pairs, columns), jnp.bfloat16),
@@ -139,15 +209,16 @@
             pltpu.VMEM((4, chunks, rows, width), jnp.float32),
             pltpu.VMEM((KINDS, chunks, rows, width), jnp.bfloat16),
             pltpu.VMEM((KINDS, chunks, rows, width), jnp.bfloat16),
-            pltpu.SemaphoreType.DMA,
             pltpu.SemaphoreType.DMA((chunks,)),
             pltpu.SemaphoreType.DMA((KINDS, chunks)),
             pltpu.SemaphoreType.DMA((KINDS, chunks)),
+            pltpu.SemaphoreType.DMA((len(HOPS), parts)),
+            pltpu.SemaphoreType.DMA((len(HOPS), parts)),
         ],
         compiler_params=pltpu.CompilerParams(
             collective_id=0, has_side_effects=True, vmem_limit_bytes=60 * 1024 * 1024
         ),
-    )(tau, integrals, row_symmetry, column_symmetry)
+    )(own, integrals, row_symmetry, column_symmetry)
 
 
 def on_device(amplitudes, singles, pair_list, irrep, block_sizes, tile_of_slot, integrals):
@@ -164,7 +235,6 @@
     right = jnp.take(singles, pair_list[:, 1], axis=0)
     combined = amplitudes + (left[:, :, None] * right[:, None, :]).reshape(local_pairs, columns)
     combined_low = combined.astype(jnp.bfloat16)
-    piece = lax.all_gather(combined_low, "ab", axis=0, tiled=True)
     slab_irrep = lax.dynamic_slice_in_dim(irrep, slab_index * slab, slab, 0)
     column_irrep = jnp.bitwise_xor(slab_irrep[:, None], irrep[None, :]).reshape(1, columns)
     capacity = tile_of_slot.shape[0] // groups
@@ -174,11 +244,11 @@
     symmetry = tile_symmetry(tiles, jnp.arange(tile_rows, dtype=jnp.int32), irrep)
     live = jnp.arange(capacity, dtype=jnp.int32)[:, None] < count
     symmetry = jnp.where(live, symmetry, -1).reshape(capacity * tile_rows, 1)
-    width = min(512, tile_rows // 2)
+    width = min(256, tile_rows // 2)
     return ladder(
-        ring, piece, integrals,
+        ring, combined_low, integrals,
         symmetry.astype(jnp.bfloat16), column_irrep.astype(jnp.bfloat16),
-        width, min(256, width),
+        width, min(256, width), 2,
     )
 
 

time: 148 us -> 121 us (0.82)
  waiting for transfers between devices: 27.5 us -> 0 us
  Pallas kernels: 86.9 us -> 108 us
  between operations: 14.2 us -> 0.65 us
  local copies, waits for them, and re-layouts: 16.4 us -> 8.73 us
    all_gather x1 -> x0, waiting for transfers between devices: 27.5 us -> none  [on_device(): piece = lax.all_gather(combined_low, 'ab', axis=0, tiled=True)]
    pallas_call x1, Pallas kernels: 86.9 us -> 108 us  [ladder(): pl.pallas_call(functools.partial(ladder_kernel, ring, width, inner, parts...]
    gather x1 -> x0, local copies, waits for them, and re-layouts: 8.58 us -> none  [tile_symmetry(): trailing = jnp.take(irrep, rows % orbitals)]
    unnamed x15 -> x10, local copies, waits for them, and re-layouts: 5.72 us -> 5.29 us
  transfers between devices with their start and end apart: 1 -> 0, of which waited for: 1 -> 0; matrix products, arithmetic and copies ran while one was open for 8% -> 0% of each run, Pallas kernels for 0% -> 0%
where the time goes in v2:
time: 121 us
  Pallas kernels  108 us (89%)
  local copies, waits for them, and re-layouts  8.73 us (7%)
  other arithmetic  3.73 us (3%)
    pallas_call x1, Pallas kernels, ladder(): pl.pallas_call(functools.partial(ladder_kernel, ring, width, inner, parts...  108 us
    unnamed x10, local copies, waits for them, and re-layouts  5.29 us

profile of v2, /device:TPU:0, one launch (start us, length us, event | category | flops | bytes accessed | tf_op | source)
XLA Modules:
  0.0 120.7 jit_solution(2649220343500669990)
XLA Ops:
  0.0 0.0 copy-start
  0.0 1.3 %dynamic-slice.2 = s32[1]{0:T(128)} dynamic-slice(s32[16]{0:T(128)} %param.13, s32[]{:T(128)S(6)} %select_n.66), dynamic_slice_sizes={1} | dynamic-slice | bytes 12 | solution.py:242
  1.9 0.8 dynamic_slice.11
  2.7 0.7 broadcast_add_fusion
  3.4 0.8 compare_and_fusion.1
  4.2 0.9 fusion.7
  5.1 0.6 copy.13
  5.7 0.1 fusion
  5.8 0.0 copy-done
  5.8 0.7 gather_fusion.1
  6.5 0.1 broadcast_select_fusion
  6.6 0.0 copy-start.1
  6.6 0.7 gather_fusion
  7.3 0.1 dynamic-slice_select_fusion
  7.4 0.2 broadcast_multiply_fusion
  7.6 0.2 copy.9
  7.8 0.0 copy-done.1
  7.8 0.8 add_convert_fusion.own_ref
  8.6 1.4 %copy.12 = bf16[1,4096]{0,1:T(8,128)(2,1)} copy(bf16[1,4096]{1,0:T(2,128)(2,1)S(1)} %bitcast.27) | data formatting | bytes 16384
  10.0 107.5 %shard_map.73 = f32[128,4096]{1,0:T(8,128)} custom-call(bf16[64,2048]{1,0:T(8,128)(2,1)} %add_convert_fusion.own_ref, bf16[4096,2048]{1,0:T(8,128)(2,1)} %tiles_any.1, bf16[4096,1]{1,0:T(8,128)(2,1)} %bitcast.24, bf16[1,2048]{1,0:T(2,128)(2,1)} %bitcast.28), custom_call_target="tpu_custom_call" | custom-call | tf_op jit(solution)/shard_map/pallas_call | solution.py:200
  117.6 3.1 %copy.17 = f32[128,4096]{1,0:T(8,128)} copy(f32[128,4096]{1,0:T(8,128)} %shard_map.73) | data formatting | bytes 4194304
  (5 shorter events, 0.0 us)
Async XLA Ops:
  0.0 5.8 %copy-start = (f32[256,1024]{1,0:T(8,128)S(1)}, f32[256,1024]{1,0:T(8,128)}, u32[]{:S(2)}) copy-start(f32[256,1024]{1,0:T(8,128)} %param.10) | copy-start | bytes 3145732
  6.6 1.2 copy-start.1

commit v3 on v2

--- a/solution.py
+++ b/solution.py
@@ -29,21 +29,10 @@
 RELAYS = ((0, (4, 5, 6)), (1, (7, 8)), (2, (9,)), (4, (10,)), (5, (11, 12)), (7, (13,)), (11, (14,)))
 
 
-def tile_symmetry(tiles, rows, irrep):
-    orbitals = irrep.shape[0]
-    table = jnp.arange(orbitals, dtype=jnp.int32)
-    first = jnp.sum(jnp.where(table[None, :] == 2 * tiles[:, None], irrep[None, :], 0), axis=1)
-    second = jnp.sum(jnp.where(table[None, :] == 2 * tiles[:, None] + 1, irrep[None, :], 0), axis=1)
-    upper = (rows // orbitals)[None, :]
-    leading = jnp.where(upper == 0, first[:, None], second[:, None])
-    trailing = jnp.tile(irrep, rows.shape[0] // orbitals)
-    return jnp.bitwise_xor(leading, trailing[None, :])
-
-
 def ladder_kernel(
     ring, width, inner, parts,
-    own_ref, tiles_any, row_ref, column_ref, out_ref,
-    tau, tiles, acc, keep, sent, held,
+    amplitudes_ref, singles_ref, table_ref, pairs_ref, irrep_ref, sizes_ref, slots_ref, tiles_any, out_ref,
+    tau, tiles, acc, keep, sent, held, own_ref, right, left, trailing, column,
     tile_sem, send_sem, recv_sem, spread_sem, gather_sem,
 ):
     chunks = tiles.shape[0]
@@ -114,13 +103,38 @@
         pl.semaphore_signal(barrier, inc=1, device_id={"cd": other}, device_id_type=MESH)
     for other in (beside, above, below, twin):
         pl.semaphore_signal(barrier, inc=1, device_id={"ab": other}, device_id_type=MESH)
-    pl.semaphore_wait(barrier, 7)
-
-    for hop in (1, 2, 0, 3):
-        for part in range(parts):
-            give(hop, part).start()
+
+    orbitals = singles_ref.shape[1]
+    slab = tau.shape[1] // orbitals
+    capacity = tiles.shape[0] * width // (2 * orbitals)
+
+    occupied = lax.broadcasted_iota(jnp.int32, (own_ref.shape[0], singles_ref.shape[0]), 1)
+    for ref, at in ((left, 0), (right, 1)):
+        chosen = (occupied == pairs_ref[:, at:at + 1]).astype(jnp.float32)
+        ref[...] = jnp.dot(
+            chosen, singles_ref[:, :ref.shape[1]],
+            precision=lax.Precision.HIGHEST, preferred_element_type=jnp.float32,
+        )
+    lane = lax.broadcasted_iota(jnp.int32, left.shape, 1)
+    for k in range(slab):
+        factor = jnp.sum(jnp.where(lane == me * slab + k, left[...], 0.0), axis=1, keepdims=True)
+        span = slice(k * orbitals, (k + 1) * orbitals)
+        own_ref[:, span] = (amplitudes_ref[:, span] + factor * right[...]).astype(jnp.bfloat16)
     for part in range(parts):
         tau[block(owner, part), :] = own_ref[part * depth:(part + 1) * depth, :]
+    pl.semaphore_wait(barrier, 7)
+
+    for hop in (1, 2, 0, 3):
+        for part in range(parts):
+            give(hop, part).start()
+
+    for row in range(orbitals // 128):
+        labels = table_ref[row:row + 1, :]
+        spread = jnp.broadcast_to(labels.astype(jnp.float32), (128, 128))
+        trailing[row * 128:(row + 1) * 128, :] = spread.T
+        for k in range(slab):
+            mixed = jnp.bitwise_xor(labels, irrep_ref[me * slab + k])
+            column[:, k * orbitals + row * 128:k * orbitals + (row + 1) * 128] = mixed.astype(jnp.float32)
     for arrived, onward in RELAYS:
         for part in range(parts):
             take(arrived, part)
@@ -139,9 +153,15 @@
         @pl.loop(0, width // inner)
         def _(t):
             at = pl.multiple_of(t * inner, inner)
-            row = row_ref[pl.ds(pl.multiple_of(c * width + t * inner, inner), inner), :]
+            start = c * width + t * inner
+            slot = lax.div(start, 2 * orbitals)
+            upper = lax.rem(lax.div(start, orbitals), 2)
+            leading = irrep_ref[2 * slots_ref[owner * capacity + slot] + upper]
+            label = trailing[pl.ds(pl.multiple_of(lax.rem(start, orbitals), inner), inner), 0:1]
+            mixed = jnp.bitwise_xor(label.astype(jnp.int32), leading)
+            row = jnp.where(slot < sizes_ref[owner], mixed, -1).astype(jnp.float32).astype(jnp.bfloat16)
             tile = tiles[c, pl.ds(at, inner), :]
-            masked = jnp.where(row == column_ref[...], tile, jnp.zeros_like(tile))
+            masked = jnp.where(row == column[...].astype(jnp.bfloat16), tile, jnp.zeros_like(tile))
             acc[:, pl.ds(at, inner)] = lax.dot_general(
                 tau[...], masked, (((1,), (1,)), ((), ())), preferred_element_type=jnp.float32
             )
@@ -190,17 +210,24 @@
             give(hop, part).wait_send()
 
 
-def ladder(ring, own, integrals, row_symmetry, column_symmetry, width, inner, parts):
-    pairs, columns = own.shape[0] * 16, own.shape[1]
+def on_device(amplitudes, singles, pair_list, irrep, block_sizes, tile_of_slot, integrals):
+    groups = lax.axis_size("ab")
+    ring = lax.axis_size("cd") // 2
+    local_pairs, columns = amplitudes.shape
+    orbitals = irrep.shape[0]
+    pairs = local_pairs * groups
     rows = pairs // (2 * ring)
     total = integrals.shape[0]
+    width = min(256, orbitals)
+    parts = 2
     chunks = total // width
     anywhere = pl.BlockSpec(memory_space=pl.ANY)
     local = pl.BlockSpec(memory_space=pltpu.VMEM)
+    scalars = pl.BlockSpec(memory_space=pltpu.SMEM)
     return pl.pallas_call(
-        functools.partial(ladder_kernel, ring, width, inner, parts),
+        functools.partial(ladder_kernel, ring, width, min(256, width), parts),
         out_shape=jax.ShapeDtypeStruct((rows, total), jnp.float32),
-        in_specs=[local, anywhere, local, local],
+        in_specs=[local, local, local, local, scalars, scalars, scalars, anywhere],
         out_specs=local,
         scratch_shapes=[
             pltpu.VMEM((pairs, columns), jnp.bfloat16),
@@ -209,6 +236,11 @@
             pltpu.VMEM((4, chunks, rows, width), jnp.float32),
             pltpu.VMEM((KINDS, chunks, rows, width), jnp.bfloat16),
             pltpu.VMEM((KINDS, chunks, rows, width), jnp.bfloat16),
+            pltpu.VMEM((local_pairs, columns), jnp.bfloat16),
+            pltpu.VMEM((local_pairs, orbitals), jnp.float32),
+            pltpu.VMEM((local_pairs, 128), jnp.float32),
+            pltpu.VMEM((orbitals, 128), jnp.float32),
+            pltpu.VMEM((1, columns), jnp.float32),
             pltpu.SemaphoreType.DMA((chunks,)),
             pltpu.SemaphoreType.DMA((KINDS, chunks)),
             pltpu.SemaphoreType.DMA((KINDS, chunks)),
@@ -218,37 +250,9 @@
         compiler_params=pltpu.CompilerParams(
             collective_id=0, has_side_effects=True, vmem_limit_bytes=60 * 1024 * 1024
         ),
-    )(own, integrals, row_symmetry, column_symmetry)
-
-
-def on_device(amplitudes, singles, pair_list, irrep, block_sizes, tile_of_slot, integrals):
-    groups = lax.axis_size("ab")
-    ring = lax.axis_size("cd") // 2
-    owner_index = lax.axis_index("ab")
-    slab_index = lax.axis_index("cd")
-    orbitals = irrep.shape[0]
-    columns = amplitudes.shape[1]
-    slab = columns // orbitals
-    local_pairs = amplitudes.shape[0]
-    left = jnp.take(singles, pair_list[:, 0], axis=0)
-    left = lax.dynamic_slice_in_dim(left, slab_index * slab, slab, 1)
-    right = jnp.take(singles, pair_list[:, 1], axis=0)
-    combined = amplitudes + (left[:, :, None] * right[:, None, :]).reshape(local_pairs, columns)
-    combined_low = combined.astype(jnp.bfloat16)
-    slab_irrep = lax.dynamic_slice_in_dim(irrep, slab_index * slab, slab, 0)
-    column_irrep = jnp.bitwise_xor(slab_irrep[:, None], irrep[None, :]).reshape(1, columns)
-    capacity = tile_of_slot.shape[0] // groups
-    tile_rows = integrals.shape[0] // capacity
-    count = jnp.take(block_sizes, owner_index)
-    tiles = lax.dynamic_slice_in_dim(tile_of_slot, owner_index * capacity, capacity, 0)
-    symmetry = tile_symmetry(tiles, jnp.arange(tile_rows, dtype=jnp.int32), irrep)
-    live = jnp.arange(capacity, dtype=jnp.int32)[:, None] < count
-    symmetry = jnp.where(live, symmetry, -1).reshape(capacity * tile_rows, 1)
-    width = min(256, tile_rows // 2)
-    return ladder(
-        ring, combined_low, integrals,
-        symmetry.astype(jnp.bfloat16), column_irrep.astype(jnp.bfloat16),
-        width, min(256, width), 2,
+    )(
+        amplitudes, singles, irrep.reshape(orbitals // 128, 128), pair_list,
+        irrep, block_sizes, tile_of_slot, integrals,
     )
 
 

time: 121 us -> 113 us (0.934)
  local copies, waits for them, and re-layouts: 8.73 us -> 4.49 us
  other arithmetic: 3.73 us -> 0 us
    gather x2 -> x0, local copies, waits for them, and re-layouts: 1.36 us -> none  [the longest x1 0.68 us: on_device(): right = jnp.take(singles, pair_list[:, 1], axis=0)]
    another operation x1 -> x0, local copies, waits for them, and re-layouts: 1.32 us -> none  [on_device(): count = jnp.take(block_sizes, owner_index)]
    unnamed x10 -> x2, local copies, waits for them, and re-layouts: 5.29 us -> 4.49 us
where the time goes in v3:
time: 113 us; the launch traced here: 112 us
  Pallas kernels  108 us (96%)
  local copies, waits for them, and re-layouts  4.49 us (4%)
    pallas_call x1, Pallas kernels, on_device(): pl.pallas_call(functools.partial(ladder_kernel, ring, width, min(256, wid...  108 us
    unnamed x2, local copies, waits for them, and re-layouts  4.49 us

profile of v3, /device:TPU:0, one launch (start us, length us, event | category | flops | bytes accessed | tf_op | source)
XLA Modules:
  0.0 112.3 jit_solution(16417805367654112335)
XLA Ops:
  0.0 1.4 %copy.8.pairs_ref = s32[64,2]{1,0:T(8,128)} copy(s32[64,2]{0,1:T(2,128)} %param.9) | data formatting | bytes 1024 | tf_op args[2]
  1.4 107.8 %shard_map.73 = f32[128,4096]{1,0:T(8,128)} custom-call(f32[64,2048]{1,0:T(8,128)} %amplitudes_ref.1, f32[256,1024]{1,0:T(8,128)} %singles_ref.1, s32[8,128]{1,0:T(8,128)} %bitcast.1, s32[64,2]{1,0:T(8,128)} %copy.8.pairs_ref, s32[1024]{0:T(1024)} %irrep_ref.1, s32[16]{0:T(128)} %sizes_ref.1, s32[32]{0:T(128)} %slots_ref.1, bf16[4096,2048]{1,0:T(8,128)(2,1)} %tiles_any.1), custom_call_target="tpu_custom_call" | custom-call | tf_op jit(solution)/shard_map/pallas_call | solution.py:227
  109.2 3.1 %copy.10 = f32[128,4096]{1,0:T(8,128)} copy(f32[128,4096]{1,0:T(8,128)} %shard_map.73) | data formatting | bytes 4194304

commit v4 on v3

--- a/solution.py
+++ b/solution.py
@@ -9,6 +9,7 @@
 
 MESH = pl.DeviceIdType.MESH
 KINDS = 7
+LAG = 2
 HOPS = (
     ((0, 0, 0), 0, (0, 1, 0)),
     ((0, 0, 0), 1, (3, 0, 0)),
@@ -32,7 +33,7 @@
 def ladder_kernel(
     ring, width, inner, parts,
     amplitudes_ref, singles_ref, table_ref, pairs_ref, irrep_ref, sizes_ref, slots_ref, tiles_any, out_ref,
-    tau, tiles, acc, keep, sent, held, own_ref, right, left, trailing, column,
+    tau, tiles, acc, keep, sent, held, sent_far, held_far, own_ref, right, left, trailing, column,
     tile_sem, send_sem, recv_sem, spread_sem, gather_sem,
 ):
     chunks = tiles.shape[0]
@@ -93,6 +94,31 @@
             device_id={"cd": targets[kind]},
             device_id_type=MESH,
         )
+
+    half = rows // 2
+
+    def remote_half(kind, c):
+        return pltpu.make_async_remote_copy(
+            src_ref=sent.at[kind, c, pl.ds(0, half), :],
+            dst_ref=held.at[kind, c, pl.ds(0, half), :],
+            send_sem=send_sem.at[kind, c],
+            recv_sem=recv_sem.at[kind, c],
+            device_id={"cd": targets[kind]},
+            device_id_type=MESH,
+        )
+
+    def remote_far(c):
+        return pltpu.make_async_remote_copy(
+            src_ref=sent_far.at[lax.div(c, 2)],
+            dst_ref=held_far.at[lax.div(c, 2)],
+            send_sem=send_sem.at[6, c],
+            recv_sem=recv_sem.at[6, c],
+            device_id={"cd": across},
+            device_id_type=MESH,
+        )
+
+    def across_first(c):
+        return (lax.rem(c, 2) == 1) & (c < chunks - 2)
 
     @pl.loop(0, chunks)
     def _(c):
@@ -166,11 +192,22 @@
                 tau[...], masked, (((1,), (1,)), ((), ())), preferred_element_type=jnp.float32
             )
 
-        for kind, part, block in ((0, 0, far_y), (1, 1, far_y), (2, 1, up_y), (3, 0, down_y)):
-            sent[kind, c] = piece(part, block).astype(jnp.bfloat16)
-            remote(kind, c).start()
-        for slot, part, block in ((0, 0, up_y), (1, 1, down_y), (2, 0, y), (3, 1, y)):
-            keep[slot, c] = piece(part, block)
+        @pl.when(across_first(c))
+        def _():
+            for step in range(4):
+                at_y = lax.rem(y + step, ring)
+                sent_far[lax.div(c, 2), step] = piece(1 - x, at_y).astype(jnp.bfloat16)
+            remote_far(c).start()
+            for step in range(4):
+                keep[step, c] = piece(x, lax.rem(y + step, ring))
+
+        @pl.when(jnp.logical_not(across_first(c)))
+        def _():
+            for kind, part, block in ((0, 0, far_y), (1, 1, far_y), (2, 1, up_y), (3, 0, down_y)):
+                sent[kind, c] = piece(part, block).astype(jnp.bfloat16)
+                remote(kind, c).start()
+            for slot, part, block in ((0, 0, up_y), (1, 1, down_y), (2, 0, y), (3, 1, y)):
+                keep[slot, c] = piece(part, block)
 
     def relay(c):
         for kind in (0, 1):
@@ -193,17 +230,66 @@
         at = pl.multiple_of(c * width, width)
         out_ref[:, pl.ds(at, width)] = keep[2, c] + held[6, c].astype(jnp.float32)
 
-    @pl.loop(0, chunks + 3)
+    low, high = slice(0, half), slice(half, rows)
+
+    def fan(c):
+        remote_far(c).wait_recv()
+
+        def total(step, span):
+            return keep[step, c, span, :] + held_far[lax.div(c, 2), step, span, :].astype(jnp.float32)
+
+        for kind, step, span in ((0, 2, low), (1, 2, high), (2, 1, high), (3, 3, low)):
+            sent[kind, c, 0:half, :] = total(step, span).astype(jnp.bfloat16)
+            remote_half(kind, c).start()
+        for step, span in ((1, low), (3, high), (0, low), (0, high)):
+            keep[step, c, span, :] = total(step, span)
+
+    def relay_half(c):
+        for kind, step, span in ((0, 1, low), (1, 3, high)):
+            remote_half(kind, c).wait_recv()
+            total = keep[step, c, span, :] + held[kind, c, 0:half, :].astype(jnp.float32)
+            sent[4 + kind, c, 0:half, :] = total.astype(jnp.bfloat16)
+            remote_half(4 + kind, c).start()
+
+    def finish_half(c):
+        for kind in (2, 3, 4, 5):
+            remote_half(kind, c).wait_recv()
+        at = pl.multiple_of(c * width, width)
+        for direct, relayed, span in ((3, 4, low), (2, 5, high)):
+            near = held[direct, c, 0:half, :].astype(jnp.float32)
+            out_ref[span, pl.ds(at, width)] = keep[0, c, span, :] + near + held[relayed, c, 0:half, :].astype(jnp.float32)
+
+    @pl.loop(0, chunks + 3 * LAG)
     def _(i):
-        for lag, stage in enumerate((multiply, relay, cross, finish)):
-            @pl.when((i >= lag) & (i < chunks + lag))
+        @pl.when(i < chunks)
+        def _():
+            multiply(i)
+
+        for order, pair in enumerate(((relay, fan), (cross, relay_half), (finish, finish_half))):
+            lag = LAG * (order + 1)
+            c = i - lag
+            inside = (i >= lag) & (c < chunks)
+
+            @pl.when(inside & across_first(c))
             def _():
-                stage(i - lag)
+                pair[1](c)
+
+            @pl.when(inside & jnp.logical_not(across_first(c)))
+            def _():
+                pair[0](c)
 
     @pl.loop(0, chunks)
     def _(c):
-        for kind in range(KINDS):
-            remote(kind, c).wait_send()
+        @pl.when(across_first(c))
+        def _():
+            remote_far(c).wait_send()
+            for kind in range(6):
+                remote_half(kind, c).wait_send()
+
+        @pl.when(jnp.logical_not(across_first(c)))
+        def _():
+            for kind in range(KINDS):
+                remote(kind, c).wait_send()
 
     for hop in range(len(HOPS)):
         for part in range(parts):
@@ -236,6 +322,8 @@
             pltpu.VMEM((4, chunks, rows, width), jnp.float32),
             pltpu.VMEM((KINDS, chunks, rows, width), jnp.bfloat16),
             pltpu.VMEM((KINDS, chunks, rows, width), jnp.bfloat16),
+            pltpu.VMEM((chunks // 2, ring, rows, width), jnp.bfloat16),
+            pltpu.VMEM((chunks // 2, ring, rows, width), jnp.bfloat16),
             pltpu.VMEM((local_pairs, columns), jnp.bfloat16),
             pltpu.VMEM((local_pairs, orbitals), jnp.float32),
             pltpu.VMEM((local_pairs, 128), jnp.float32),

time: 113 us -> 104 us (0.920)
  Pallas kernels: 108 us -> 97.9 us
    pallas_call x1, Pallas kernels: 108 us -> 97.9 us  [on_device(): pl.pallas_call(functools.partial(ladder_kernel, ring, width, min(256, wid...]
where the time goes in v4:
time: 104 us; the launch traced here: 102 us
  Pallas kernels  97.9 us (94%)
  local copies, waits for them, and re-layouts  4.49 us (4%)
    pallas_call x1, Pallas kernels, on_device(): pl.pallas_call(functools.partial(ladder_kernel, ring, width, min(256, wid...  97.9 us
    unnamed x2, local copies, waits for them, and re-layouts  4.49 us

profile of v4, /device:TPU:0, one launch (start us, length us, event | category | flops | bytes accessed | tf_op | source)
XLA Modules:
  0.0 102.4 jit_solution(2210313380540150134)
XLA Ops:
  0.0 1.4 %copy.8.pairs_ref = s32[64,2]{1,0:T(8,128)} copy(s32[64,2]{0,1:T(2,128)} %param.9) | data formatting | bytes 1024 | tf_op args[2]
  1.4 97.9 %shard_map.73 = f32[128,4096]{1,0:T(8,128)} custom-call(f32[64,2048]{1,0:T(8,128)} %amplitudes_ref.1, f32[256,1024]{1,0:T(8,128)} %singles_ref.1, s32[8,128]{1,0:T(8,128)} %bitcast.1, s32[64,2]{1,0:T(8,128)} %copy.8.pairs_ref, s32[1024]{0:T(1024)} %irrep_ref.1, s32[16]{0:T(128)} %sizes_ref.1, s32[32]{0:T(128)} %slots_ref.1, bf16[4096,2048]{1,0:T(8,128)(2,1)} %tiles_any.1), custom_call_target="tpu_custom_call" | custom-call | tf_op jit(solution)/shard_map/pallas_call | solution.py:313
  99.2 3.1 %copy.10 = f32[128,4096]{1,0:T(8,128)} copy(f32[128,4096]{1,0:T(8,128)} %shard_map.73) | data formatting | bytes 4194304

commit v5 on v4

--- a/solution.py
+++ b/solution.py
@@ -9,7 +9,7 @@
 
 MESH = pl.DeviceIdType.MESH
 KINDS = 7
-LAG = 2
+LAG = 8
 HOPS = (
     ((0, 0, 0), 0, (0, 1, 0)),
     ((0, 0, 0), 1, (3, 0, 0)),

time: 104 us -> 96.7 us (0.930)
  Pallas kernels: 97.9 us -> 90.8 us
    pallas_call x1, Pallas kernels: 97.9 us -> 90.8 us  [on_device(): pl.pallas_call(functools.partial(ladder_kernel, ring, width, min(256, wid...]
where the time goes in v5:
time: 96.7 us; the launch traced here: 95.3 us
  Pallas kernels  90.8 us (94%)
  local copies, waits for them, and re-layouts  4.49 us (5%)
    pallas_call x1, Pallas kernels, on_device(): pl.pallas_call(functools.partial(ladder_kernel, ring, width, min(256, wid...  90.8 us
    unnamed x2, local copies, waits for them, and re-layouts  4.49 us

profile of v5, /device:TPU:0, one launch (start us, length us, event | category | flops | bytes accessed | tf_op | source)
XLA Modules:
  0.0 95.3 jit_solution(12363957540835453544)
XLA Ops:
  0.0 1.4 %copy.8.pairs_ref = s32[64,2]{1,0:T(8,128)} copy(s32[64,2]{0,1:T(2,128)} %param.9) | data formatting | bytes 1024 | tf_op args[2]
  1.4 90.8 %shard_map.73 = f32[128,4096]{1,0:T(8,128)} custom-call(f32[64,2048]{1,0:T(8,128)} %amplitudes_ref.1, f32[256,1024]{1,0:T(8,128)} %singles_ref.1, s32[8,128]{1,0:T(8,128)} %bitcast.1, s32[64,2]{1,0:T(8,128)} %copy.8.pairs_ref, s32[1024]{0:T(1024)} %irrep_ref.1, s32[16]{0:T(128)} %sizes_ref.1, s32[32]{0:T(128)} %slots_ref.1, bf16[4096,2048]{1,0:T(8,128)(2,1)} %tiles_any.1), custom_call_target="tpu_custom_call" | custom-call | tf_op jit(solution)/shard_map/pallas_call | solution.py:313
  92.2 3.1 %copy.10 = f32[128,4096]{1,0:T(8,128)} copy(f32[128,4096]{1,0:T(8,128)} %shard_map.73) | data formatting | bytes 4194304
